TPU v7x, 32 devices: a whole 2x2x4 slice. The times are simulated.
32 devices in a mesh: seq: 8 (over y, x, core), head: 4 (over z).
Axes of the slice: x: 2, y: 2, z: 4, core: 2. Of those that a mesh axis runs over, the one named last changes fastest.
Arguments:
- hidden_in: float32 [4096, 768], P('seq'), may hold values from -6 to 6
- grad_out: float32 [4096, 768], P('seq'), may hold values from -6 to 6
- doc_lengths: int32 [3], replicated, may hold values from 1 to 2048, as said below
- norm_gain: float32 [2, 768], replicated, may hold values from 0.5 to 1.5
- proj_z: float32 [2, 768, 1536], P(None, 'seq', 'head'), may hold values from -0.21875 to 0.21875
- proj_x: float32 [2, 768, 1536], P(None, 'seq', 'head'), may hold values from -0.21875 to 0.21875
- proj_bc: float32 [2, 768, 256], P(None, 'seq', 'head'), may hold values from -0.21875 to 0.21875
- proj_dt: float32 [2, 768, 24], P(None, 'seq', 'head'), may hold values from -0.21875 to 0.21875
- conv_x_kernel: float32 [2, 4, 1536], P(None, None, 'head'), may hold values from -3 to 3
- conv_x_bias: float32 [2, 1536], P(None, 'head'), may hold values from -0.5 to 0.5
- conv_bc_kernel: float32 [2, 4, 256], P(None, None, 'head'), may hold values from -3 to 3
- conv_bc_bias: float32 [2, 256], P(None, 'head'), may hold values from -0.5 to 0.5
- dt_bias: float32 [2, 24], P(None, 'head'), may hold values from -6 to -3
- a_log: float32 [2, 24], P(None, 'head'), may hold values from -3 to 2
- skip_gain: float32 [2, 24], P(None, 'head'), may hold values from 0.5 to 1.5
- gate_gain: float32 [2, 1536], P(None, 'head'), may hold values from 0.5 to 1.5
- proj_out: float32 [2, 768, 1536], P(None, 'seq', 'head'), may hold values from -0.15625 to 0.15625
Outputs:
- hidden_out: float32 [4096, 768], P('seq')
- grad_hidden: float32 [4096, 768], P('seq')
- grad_norm_gain: float32 [2, 768], replicated
- grad_proj_z: float32 [2, 768, 1536], P(None, 'seq', 'head')
- grad_proj_x: float32 [2, 768, 1536], P(None, 'seq', 'head')
- grad_proj_bc: float32 [2, 768, 256], P(None, 'seq', 'head')
- grad_proj_dt: float32 [2, 768, 24], P(None, 'seq', 'head')
- grad_conv_x_kernel: float32 [2, 4, 1536], P(None, None, 'head')
- grad_conv_x_bias: float32 [2, 1536], P(None, 'head')
- grad_conv_bc_kernel: float32 [2, 4, 256], P(None, None, 'head')
- grad_conv_bc_bias: float32 [2, 256], P(None, 'head')
- grad_dt_bias: float32 [2, 24], P(None, 'head')
- grad_a_log: float32 [2, 24], P(None, 'head')
- grad_skip_gain: float32 [2, 24], P(None, 'head')
- grad_gate_gain: float32 [2, 1536], P(None, 'head')
- grad_proj_out: float32 [2, 768, 1536], P(None, 'seq', 'head')
Inputs may be any that keep to these rules, and one draw needn't show every extreme that they name: `doc_lengths`: the 3 lengths sum to 4096, and the longest is exactly 2048.
All inputs are finite; a program needn't handle non-finite values.
Results may differ from a plain program's by a relative error of at most 0.0003.
Values sent between devices are 32-bit elements; how exact they have to be, the bound alone decides.
A program may use at most 192 MiB of HBM per device.

v0:
```python
from functools import partial

import jax
import jax.numpy as jnp
from jax import lax
from jax.sharding import PartitionSpec as P

STATE = 128
KERNEL = 4
BLOCK = 256
INNER = 1536


EPS = 1e-05
NEG_FILL = -1e30


def passed_along(array, axis, by):
    count = lax.axis_size(axis)
    pairs = [(i, i + by) for i in range(count) if 0 <= i + by < count]
    return lax.ppermute(array, axis, pairs)


def entering(value, axis, join, neutral, backward):
    count, mine = (lax.axis_size(axis), lax.axis_index(axis))
    pieces = jax.tree.map(lambda part: lax.all_gather(part, axis), value)
    if backward:
        pieces = jax.tree.map(lambda part: part[::-1], pieces)
        mine = count - 1 - mine
    running = jax.tree.map(
        lambda part, zero: jnp.full_like(part, 0) + jnp.asarray(zero, part.dtype), value, neutral
    )

    def hop(position, running):
        longer = join(running, jax.tree.map(lambda part: part[position], pieces))
        return jax.tree.map(lambda new, old: jnp.where(position < mine, new, old), longer, running)

    return lax.fori_loop(0, count - 1, hop, running)


def matmul_high(left, right):
    return jnp.dot(left, right, precision=lax.Precision.HIGHEST, preferred_element_type=jnp.float32)


def swish_act(values):
    return values * jax.nn.sigmoid(values)


def rms_scale(values):
    return lax.rsqrt(jnp.mean(values * values, axis=-1, keepdims=True) + EPS)


def segment_ids(doc_lengths, positions):
    ends = jnp.cumsum(doc_lengths)
    starts = ends - doc_lengths
    return jnp.sum((positions[:, None] >= starts[None, :]).astype(jnp.int32), axis=1) - 1


def decay_rates(dt_raw, dt_bias, a_log):
    step_size = jax.nn.softplus(dt_raw + dt_bias)
    return (step_size, -step_size * jnp.exp(a_log))


def block_step(state, seg_prev, values, step_size, log_decay, b_matrix, c_matrix, seg_now):
    count, width = values.shape
    heads = step_size.shape[1]
    head_dim = width // heads
    cum_decay = jnp.cumsum(log_decay, axis=0)
    order = jnp.arange(count)
    allowed = (order[:, None] >= order[None, :]) & (seg_now[:, None] == seg_now[None, :])
    spans = cum_decay.T[:, :, None] - cum_decay.T[:, None, :]
    decays = jnp.exp(jnp.where(allowed[None], spans, NEG_FILL))
    intersection = matmul_high(c_matrix, b_matrix.T)
    scores = decays * intersection[None] * step_size.T[:, None, :]
    per_head = values.reshape(count, heads, head_dim)
    output = jnp.einsum("hts,shp->thp", scores, per_head, precision=lax.Precision.HIGHEST).reshape(
        count, width
    )
    enter = jnp.exp(cum_decay) * (seg_now == seg_prev).astype(jnp.float32)[:, None]
    output = output + jnp.repeat(enter, head_dim, axis=1) * matmul_high(c_matrix, state.T)
    keep_end = (seg_now == seg_now[-1]).astype(jnp.float32)
    weight_end = jnp.exp(cum_decay[-1][None, :] - cum_decay) * step_size * keep_end[:, None]
    weighted = values * jnp.repeat(weight_end, head_dim, axis=1)
    carry = jnp.exp(cum_decay[-1]) * (seg_now[-1] == seg_prev).astype(jnp.float32)
    state = state * jnp.repeat(carry, head_dim)[:, None] + jnp.einsum(
        "tc,tn->cn", weighted, b_matrix, precision=lax.Precision.HIGHEST
    )
    return (state, seg_now[-1], output)


def front_fn(hidden, gain, weight_cat, inner_loc, bc_loc):
    normed = hidden * rms_scale(hidden) * gain[None, :]
    projected = matmul_high(normed, weight_cat)
    split_b = 2 * inner_loc + bc_loc
    return (projected[:, :inner_loc], projected[:, inner_loc:split_b], projected[:, split_b:])


def conv_local(raw, prev_tail, kernel, bias, seg_ext, seg_now):
    extended = jnp.concatenate([prev_tail, raw], axis=0)
    count = raw.shape[0]
    total = jnp.zeros_like(raw) + bias[None, :]
    for offset in range(KERNEL):
        keep = (seg_ext[offset : offset + count] == seg_now).astype(jnp.float32)
        total = total + kernel[offset][None, :] * extended[offset : offset + count] * keep[:, None]
    return swish_act(total)


def chain_fn(values, dt_raw, dt_bias, a_log, bc_full, seg_now, seg_prev):
    step_size, log_decay = decay_rates(dt_raw, dt_bias, a_log)
    cum_decay = jnp.cumsum(log_decay, axis=0)
    head_dim = values.shape[1] // step_size.shape[1]
    keep_end = (seg_now == seg_now[-1]).astype(jnp.float32)
    weight_end = jnp.exp(cum_decay[-1][None, :] - cum_decay) * step_size * keep_end[:, None]
    weighted = values * jnp.repeat(weight_end, head_dim, axis=1)
    state_end = jnp.einsum(
        "tc,tn->cn", weighted, bc_full[:, :STATE], precision=lax.Precision.HIGHEST
    )
    decay_end = jnp.exp(cum_decay[-1]) * (seg_now[-1] == seg_prev).astype(jnp.float32)
    return (state_end, decay_end)


def out_fn(
    values, dt_raw, dt_bias, a_log, bc_full, state_in, skip_gain, seg_now, seg_prev, block_rows
):
    step_size, log_decay = decay_rates(dt_raw, dt_bias, a_log)
    count = values.shape[0]
    state = state_in
    seg_last = seg_prev
    outputs = []
    for start in range(0, count, block_rows):
        piece = slice(start, start + block_rows)
        state, seg_last, output = block_step(
            state,
            seg_last,
            values[piece],
            step_size[piece],
            log_decay[piece],
            bc_full[piece, :STATE],
            bc_full[piece, STATE:],
            seg_now[piece],
        )
        outputs.append(output)
    head_dim = values.shape[1] // step_size.shape[1]
    return jnp.concatenate(outputs, axis=0) + jnp.repeat(skip_gain, head_dim)[None, :] * values


def gate_fn(mixed, gate_in):
    gated = mixed * swish_act(gate_in)
    return (gated, jnp.sum(gated * gated, axis=1))


def tail_fn(gated, total_sq, gate_gain, proj_out_loc):
    scale = lax.rsqrt(total_sq / INNER + EPS)
    normed_out = gated * scale[:, None] * gate_gain[None, :]
    return jnp.einsum("tc,dc->td", normed_out, proj_out_loc, precision=lax.Precision.HIGHEST)


def chain_combine(earlier, later):
    decay_first, state_first = earlier
    decay_second, state_second = later
    head_dim = state_first.shape[-2] // decay_first.shape[-1]
    return (
        decay_first * decay_second,
        state_first * jnp.repeat(decay_second, head_dim, axis=-1)[..., None] + state_second,
    )


def fetch_weights(parts):
    return (
        lax.all_gather(parts[0], "seq", axis=1, tiled=True),
        lax.all_gather(parts[1], "seq", axis=1, tiled=True),
        lax.all_gather(parts[2], "seq", axis=1, tiled=True),
        lax.all_gather(parts[3], "seq", axis=1, tiled=True),
        lax.all_gather(parts[4], "seq", axis=1, tiled=True),
    )


def spread_grads(parts):
    return (
        lax.psum_scatter(parts[0], "seq", scatter_dimension=1, tiled=True),
        lax.psum_scatter(parts[1], "seq", scatter_dimension=1, tiled=True),
        lax.psum_scatter(parts[2], "seq", scatter_dimension=1, tiled=True),
        lax.psum_scatter(parts[3], "seq", scatter_dimension=1, tiled=True),
        lax.psum_scatter(parts[4], "seq", scatter_dimension=1, tiled=True),
    )


def body(
    hidden_in,
    grad_out,
    doc_lengths,
    norm_gain,
    proj_z,
    proj_x,
    proj_bc,
    proj_dt,
    conv_x_kernel,
    conv_x_bias,
    conv_bc_kernel,
    conv_bc_bias,
    dt_bias,
    a_log,
    skip_gain,
    gate_gain,
    proj_out,
):
    count = hidden_in.shape[0]
    inner_loc = proj_z.shape[2]
    bc_loc = proj_bc.shape[2]
    margin = KERNEL - 1
    layers = proj_z.shape[0]
    positions = lax.axis_index("seq") * count + jnp.arange(-margin, count, dtype=jnp.int32)
    seg_ext = segment_ids(doc_lengths, positions)
    seg_now = seg_ext[margin:]
    seg_prev = seg_ext[margin - 1]
    stacked = (proj_z, proj_x, proj_bc, proj_dt, proj_out)
    hidden = hidden_in
    saved = []
    for layer_idx in range(layers):
        fetched = tuple(
            (
                tensor[0]
                for tensor in fetch_weights(
                    tuple((tensor[layer_idx : layer_idx + 1] for tensor in stacked))
                )
            )
        )
        full_z, full_x, full_bc, full_dt, full_out = fetched
        weight_cat = jnp.concatenate([full_z, full_x, full_bc, full_dt], axis=1)
        front_out, pull_front = jax.vjp(
            partial(front_fn, inner_loc=inner_loc, bc_loc=bc_loc),
            hidden,
            norm_gain[layer_idx],
            weight_cat,
        )
        gate_in, raw_cat, dt_raw = front_out
        prev_tail = passed_along(raw_cat[count - margin :], "seq", 1)
        kernel_cat = jnp.concatenate([conv_x_kernel[layer_idx], conv_bc_kernel[layer_idx]], axis=1)
        bias_cat = jnp.concatenate([conv_x_bias[layer_idx], conv_bc_bias[layer_idx]])
        conv_out, pull_conv = jax.vjp(
            partial(conv_local, seg_ext=seg_ext, seg_now=seg_now),
            raw_cat,
            prev_tail,
            kernel_cat,
            bias_cat,
        )
        values = conv_out[:, :inner_loc]
        bc_full = lax.all_gather(conv_out[:, inner_loc:], "head", axis=1, tiled=True)
        layer_bias = dt_bias[layer_idx]
        layer_alog = a_log[layer_idx]
        chain_out, pull_chain = jax.vjp(
            partial(chain_fn, seg_now=seg_now, seg_prev=seg_prev),
            values,
            dt_raw,
            layer_bias,
            layer_alog,
            bc_full,
        )
        state_dev, decay_dev = chain_out
        identity = (jnp.ones_like(decay_dev), jnp.zeros_like(state_dev))
        _, state_in = entering((decay_dev, state_dev), "seq", chain_combine, identity, False)
        mixed, pull_out = jax.vjp(
            partial(out_fn, seg_now=seg_now, seg_prev=seg_prev, block_rows=BLOCK),
            values,
            dt_raw,
            layer_bias,
            layer_alog,
            bc_full,
            state_in,
            skip_gain[layer_idx],
        )
        gate_out, pull_gate = jax.vjp(gate_fn, mixed, gate_in)
        gated, squares = gate_out
        total_sq = lax.psum(squares, "head")
        partial_rows, pull_tail = jax.vjp(tail_fn, gated, total_sq, gate_gain[layer_idx], full_out)
        hidden = hidden + lax.psum(partial_rows, "head")
        saved.append(
            (pull_front, pull_conv, pull_chain, pull_out, pull_gate, pull_tail, decay_dev, state_in)
        )
    grad_hidden = grad_out
    layer_big = [None] * layers
    layer_small = [None] * layers
    for layer_idx in reversed(range(layers)):
        pull_front, pull_conv, pull_chain, pull_out, pull_gate, pull_tail, decay_dev, state_in = (
            saved[layer_idx]
        )
        grad_gated, grad_total, grad_ggain, grad_full_out = pull_tail(grad_hidden)
        grad_total = lax.psum(grad_total, "head")
        grad_mixed, grad_gate_in = pull_gate((grad_gated, grad_total))
        out_values, out_dt_raw, out_bias, out_alog, out_bc, grad_state_in, grad_skip = pull_out(
            grad_mixed
        )
        identity = (jnp.ones_like(decay_dev), jnp.zeros_like(grad_state_in))
        _, grad_state_end = entering(
            (decay_dev, grad_state_in), "seq", chain_combine, identity, True
        )
        heads_loc = decay_dev.shape[0]
        grad_decay = jnp.sum((grad_state_end * state_in).reshape(heads_loc, -1), axis=1)
        end_values, end_dt_raw, end_bias, end_alog, end_bc = pull_chain(
            (grad_state_end, grad_decay)
        )
        grad_bc_loc = lax.psum_scatter(out_bc + end_bc, "head", scatter_dimension=1, tiled=True)
        grad_conv_out = jnp.concatenate([out_values + end_values, grad_bc_loc], axis=1)
        grad_raw, grad_prev, grad_kernel, grad_cbias = pull_conv(grad_conv_out)
        from_right = passed_along(grad_prev, "seq", -1)
        grad_raw = grad_raw + jnp.pad(from_right, ((count - margin, 0), (0, 0)))
        grad_h_part, grad_ngain, grad_wcat = pull_front(
            (grad_gate_in, grad_raw, out_dt_raw + end_dt_raw)
        )
        grad_branch, grad_ngain = lax.psum((grad_h_part, grad_ngain), "head")
        grad_hidden = grad_hidden + grad_branch
        split_b = 2 * inner_loc
        split_c = 2 * inner_loc + bc_loc
        grad_parts = (
            grad_wcat[:, :inner_loc],
            grad_wcat[:, inner_loc:split_b],
            grad_wcat[:, split_b:split_c],
            grad_wcat[:, split_c:],
            grad_full_out,
        )
        layer_big[layer_idx] = spread_grads(tuple((part_grad[None] for part_grad in grad_parts)))
        layer_small[layer_idx] = (
            grad_ngain,
            grad_kernel[:, :inner_loc],
            grad_cbias[:inner_loc],
            grad_kernel[:, inner_loc:],
            grad_cbias[inner_loc:],
            out_bias + end_bias,
            out_alog + end_alog,
            grad_skip,
            grad_ggain,
        )
    big_grads = tuple(
        (
            jnp.concatenate([layer_big[layer_idx][member] for layer_idx in range(layers)], axis=0)
            for member in range(5)
        )
    )
    small_stack = [
        jnp.stack([layer_small[layer_idx][member] for layer_idx in range(layers)])
        for member in range(9)
    ]
    small = lax.psum(
        (
            small_stack[0],
            small_stack[1],
            small_stack[2],
            small_stack[3],
            small_stack[4],
            small_stack[5],
            small_stack[6],
            small_stack[7],
            small_stack[8],
        ),
        "seq",
    )
    return (
        hidden,
        grad_hidden,
        small[0],
        big_grads[0],
        big_grads[1],
        big_grads[2],
        big_grads[3],
        small[1],
        small[2],
        small[3],
        small[4],
        small[5],
        small[6],
        small[7],
        small[8],
        big_grads[4],
    )


def solution(mesh):
    in_specs = (
        P("seq", None),
        P("seq", None),
        P(),
        P(),
        P(None, "seq", "head"),
        P(None, "seq", "head"),
        P(None, "seq", "head"),
        P(None, "seq", "head"),
        P(None, None, "head"),
        P(None, "head"),
        P(None, None, "head"),
        P(None, "head"),
        P(None, "head"),
        P(None, "head"),
        P(None, "head"),
        P(None, "head"),
        P(None, "seq", "head"),
    )
    out_specs = (
        P("seq", None),
        P("seq", None),
        P(),
        P(None, "seq", "head"),
        P(None, "seq", "head"),
        P(None, "seq", "head"),
        P(None, "seq", "head"),
        P(None, None, "head"),
        P(None, "head"),
        P(None, None, "head"),
        P(None, "head"),
        P(None, "head"),
        P(None, "head"),
        P(None, "head"),
        P(None, "head"),
        P(None, "seq", "head"),
    )
    return jax.shard_map(body, mesh=mesh, in_specs=in_specs, out_specs=out_specs, check_vma=False)
```

profile of v0, /device:TPU:0, one launch (start us, length us, event | category | flops | bytes accessed | tf_op | source)
XLA Modules:
  0.0 1154.2 jit_solution(10109055670000457722)
XLA Ops:
  16.6 12.5 %all_gather.75 = f32[1,768,6]{2,0,1:T(1,128)} all-gather(f32[1,96,6]{2,0,1:T(1,128)S(1)} %copy.373), channel_id=1, replica_groups=mesh['seq'=8,'head'=4] {'seq'}, dimensions={1}, use_global_device_ids=true | all-gather | bytes 20736 | tf_op jit(solution)/shard_map/all_gather | solution.py:173
  29.1 11.0 all_gather.74
  43.6 21.0 %all-gather.19.cloned.1.call-done = f32[1,768,384]{2,1,0:T(8,128)} async-done(((f32[1,96,384]{2,1,0:T(8,128)}), f32[1,768,384]{2,1,0:T(8,128)}) %all-gather.19.cloned.1.call-update) | async-done | bytes 1179664 | tf_op jit(solution)/shard_map/all_gather | solution.py:171
  80.4 16.3 %all_gather.76 = f32[512,256]{0,1:T(8,128)S(1)} all-gather(f32[512,64]{0,1:T(8,128)S(1)} %slice.565), channel_id=1, replica_groups=mesh['seq'=8,'head'=4] {'head'}, dimensions={1}, use_global_device_ids=true | all-gather | bytes 655360 | tf_op jit(solution)/shard_map/all_gather | solution.py:248
  106.9 14.5 %all-gather.4 = f32[8,1,6]{2,1,0:T(1,128)} all-gather(f32[1,1,6]{2,1,0:T(1,128)} %bitcast.807), channel_id=1, replica_groups=mesh['seq'=8,'head'=4] {'seq'}, dimensions={0}, use_global_device_ids=true | all-gather | bytes 216 | tf_op jit(solution)/shard_map/all_gather | solution.py:26
  137.4 13.6 %while.56 = (s32[]{:T(128)}, f32[384,128]{1,0:T(8,128)S(1)}, s32[]{:T(128)}, f32[8,6]{1,0:T(8,128)}, f32[8,384,128]{2,1,0:T(8,128)}, /*index=5*/s32[]{:T(128)}, s32[]{:T(128)}) while((s32[]{:T(128)}, f32[384,128]{1,0:T(8,128)S(1)}, s32[]{:T(128)}, f32[8,6]{1,0:T(8,128)}, f32[8,384,128]{2,1,0:T(8,128)}, /*index=5*/s32[]{:T(128)}, ...), condition=%wide.region_8.10_spmd.clone, body=%wide.region_7.9_spmd.clone.sunk | while | flops 196612 | bytes 596153 | solution.py:38
  157.3 10.7 psum.133
  197.0 44.1 %all-reduce.67.cloned.1.call-done = f32[512,768]{1,0:T(8,128)} async-done(((f32[512,768]{1,0:T(8,128)}), f32[512,768]{1,0:T(8,128)}) %all-reduce.67.cloned.1.call-update) | async-done | bytes 1572880 | tf_op jit(solution)/shard_map/psum | solution.py:276
  242.8 23.2 %all-gather.23.cloned.1.call-done = f32[1,768,384]{2,1,0:T(8,128)} async-done(((f32[1,96,384]{2,1,0:T(8,128)}), f32[1,768,384]{2,1,0:T(8,128)}) %all-gather.23.cloned.1.call-update) | async-done | bytes 1179664 | tf_op jit(solution)/shard_map/all_gather | solution.py:170
  266.0 26.4 %all-gather.25.cloned.1.call-done = f32[1,768,384]{2,1,0:T(8,128)} async-done(((f32[1,96,384]{2,1,0:T(8,128)}), f32[1,768,384]{2,1,0:T(8,128)}) %all-gather.25.cloned.1.call-update) | async-done | bytes 1179664 | tf_op jit(solution)/shard_map/all_gather | solution.py:171
  308.9 16.4 %all_gather.85 = f32[512,256]{0,1:T(8,128)S(1)} all-gather(f32[512,64]{0,1:T(8,128)S(1)} %slice.597), channel_id=1, replica_groups=mesh['seq'=8,'head'=4] {'head'}, dimensions={1}, use_global_device_ids=true | all-gather | bytes 655360 | tf_op jit(solution)/shard_map/all_gather | solution.py:248
  335.3 13.6 %all-gather.5 = f32[8,1,6]{2,1,0:T(1,128)S(1)} all-gather(f32[1,1,6]{2,1,0:T(1,128)S(1)} %bitcast.806), channel_id=1, replica_groups=mesh['seq'=8,'head'=4] {'seq'}, dimensions={0}, use_global_device_ids=true | all-gather | bytes 216 | tf_op jit(solution)/shard_map/all_gather | solution.py:26
  359.6 13.7 %while.57 = (s32[]{:T(128)}, f32[384,128]{1,0:T(8,128)}, s32[]{:T(128)}, f32[8,6]{1,0:T(8,128)S(1)}, f32[8,384,128]{2,1,0:T(8,128)}, /*index=5*/s32[]{:T(128)}, s32[]{:T(128)}) while((s32[]{:T(128)}, f32[384,128]{1,0:T(8,128)}, s32[]{:T(128)}, f32[8,6]{1,0:T(8,128)S(1)}, f32[8,384,128]{2,1,0:T(8,128)}, /*index=5*/s32[]{:T(128)}, ...), condition=%wide.region_20.22_spmd.clone, body=%wide.region_19.21_spmd.clone.sunk | while | flops 196612 | bytes 596153 | solution.py:38
  469.0 18.6 %while.58 = (s32[]{:T(128)}, f32[384,128]{1,0:T(8,128)}, s32[]{:T(128)}, f32[8,6]{1,0:T(8,128)}, f32[8,384,128]{2,1,0:T(8,128)}, /*index=5*/s32[]{:T(128)}, s32[]{:T(128)}) while((s32[]{:T(128)}, f32[384,128]{1,0:T(8,128)}, s32[]{:T(128)}, f32[8,6]{1,0:T(8,128)}, f32[8,384,128]{2,1,0:T(8,128)}, /*index=5*/s32[]{:T(128)}, ...), condition=%wide.region_45.47_spmd.clone, body=%wide.region_44.46_spmd.clone.sunk | while | flops 196612 | bytes 596153 | solution.py:38
  534.2 68.7 %all-reduce.69.cloned.1.call-done = f32[512,768]{1,0:T(8,128)} async-done(((f32[512,768]{1,0:T(8,128)}), f32[512,768]{1,0:T(8,128)}) %all-reduce.69.cloned.1.call-update) | async-done | bytes 1572880 | tf_op jit(solution)/shard_map/psum | solution.py:310
  645.4 10.8 all-gather.35.cloned.1.call-done
  658.8 18.5 %while.59 = (s32[]{:T(128)}, f32[384,128]{1,0:T(8,128)}, s32[]{:T(128)}, f32[8,6]{1,0:T(8,128)}, f32[8,384,128]{2,1,0:T(8,128)}, /*index=5*/s32[]{:T(128)}, s32[]{:T(128)}) while((s32[]{:T(128)}, f32[384,128]{1,0:T(8,128)}, s32[]{:T(128)}, f32[8,6]{1,0:T(8,128)}, f32[8,384,128]{2,1,0:T(8,128)}, /*index=5*/s32[]{:T(128)}, ...), condition=%wide.region_76.78_spmd.clone, body=%wide.region_75.77_spmd.clone.sunk | while | flops 196612 | bytes 596153 | solution.py:38
  817.4 12.3 %multiply_reduce_fusion.1 = (f32[768]{0:T(1024)}, f32[512]{0:T(512)S(1)}, f32[512,768]{1,0:T(8,128)S(1)}) fusion(f32[512,768]{1,0:T(8,128)S(1)} %copy-done, f32[512]{0:T(512)S(1)} %copy-done.133, f32[768]{0:T(1024)S(1)} %get-tuple-element.583, f32[768,6]{1,0:T(8,128)S(1)} %bitcast.688, f32[768,64]{1,0:T(8,128)} %bitcast.690, f32[768,384]{1,0:T(8,128)} %bitcast.811, ...), kind=kOutput, calls=%fused_computation.19 | convolution fusion | flops 3959326976 | bytes 7446528 | tf_op jit(solution)/shard_map/transpose(jvp())/dot_general | solution.py:42
  832.0 22.7 %reduce-scatter.21.cloned.1.call-done = f32[1,96,384]{2,1,0:T(8,128)} async-done(((f32[1,768,384]{2,1,0:T(8,128)}), f32[1,96,384]{2,1,0:T(8,128)}) %reduce-scatter.21.cloned.1.call-update) | async-done | bytes 147472 | tf_op jit(solution)/shard_map/reduce_scatter | solution.py:184
  856.8 11.8 %all-reduce.60 = (f32[1,768]{1,0:T(1,128)S(1)}, f32[1,768]{1,0:T(1,128)S(1)}) all-reduce(f32[1,768]{1,0:T(1,128)S(1)} %copy-done.186, f32[1,768]{1,0:T(1,128)S(1)} %stack.65), channel_id=1, replica_groups=mesh['seq'=8,'head'=4] {'head'}, use_global_device_ids=true, to_apply=%region_91.93 | all-reduce | flops 1536 | bytes 12288 | tf_op jit(solution)/shard_map/psum | solution.py:310
  868.6 23.1 %all-reduce.58 = (f32[2,768]{1,0:T(2,128)}, f32[2,4,384]{2,1,0:T(4,128)}, f32[2,384]{1,0:T(2,128)}, f32[2,4,64]{2,1,0:T(4,128)}, f32[2,64]{1,0:T(2,128)}, /*inde...) all-reduce(f32[2,768]{1,0:T(2,128)S(1)} %pad_maximum_fusion.16, ...), channel_id=1, replica_groups=mesh['seq'=8,'head'=4] {'seq'}, use_global_device_ids=true, to_apply=%region_92.94 | all-reduce | flops 6820 | bytes 54560 | tf_op jit(solution)/shard_map/psum | solution.py:343
  893.2 35.3 %reduce-scatter.25.cloned.1.call-done = f32[96,64]{1,0:T(8,128)} async-done(((f32[768,64]{1,0:T(8,128)}), f32[96,64]{1,0:T(8,128)}) %reduce-scatter.25.cloned.1.call-update) | async-done | bytes 24592
  930.0 88.7 %all-reduce.71.cloned.1.call-done = (f32[1,768,384]{2,0,1:T(1,128)}, f32[1,768,384]{2,0,1:T(1,128)}, f32[1,768,384]{2,0,1:T(1,128)}, f32[1,768,384]{2,0,1:T(1,128)}) async-done(((f32[1,768,384]{2,0,1:T(1,128)}, f32[1,768,384]{2,0,1:T(1,128)}, f32[1,768,384]{2,0,1:T(1,128)}, f32[1,768,384]{2,0,1:T(1,128)}), (f32[1,768,384]{2,0,1:T(1,128)}, f32[1,768,384]{2,0,1:T(1,128)}, f32[1,768,384]{2,0,1:T(1,128)}, ...) | async-done | bytes 4718608
  1024.7 118.2 %all-reduce.73.cloned.1.call-done = (f32[512,768]{1,0:T(8,128)}, f32[512,768]{1,0:T(8,128)}) async-done(((f32[512,768]{1,0:T(8,128)}, f32[512,768]{1,0:T(8,128)}), (f32[512,768]{1,0:T(8,128)}, f32[512,768]{1,0:T(8,128)})) %all-reduce.73.cloned.1.call-update) | async-done | bytes 3145744 | tf_op jit(solution)/shard_map/psum | solution.py:276
  (1088 shorter events, 531.9 us)
Async XLA Ops:
  7.3 36.4 %all-gather.17.cloned.1.call-start = ((), (), s32[]{:S(2)}) async-start(), calls=%async_computation.8 | async-start | bytes 1327104 | tf_op jit(solution)/shard_map/all_gather | solution.py:170
  9.2 55.5 %all-gather.19.cloned.1.call-start = ((), (), s32[]{:S(2)}) async-start(), calls=%async_computation.9 | async-start | bytes 1327104 | tf_op jit(solution)/shard_map/all_gather | solution.py:171
  10.9 126.4 %all-gather.29.cloned.1.call-start = ((), (), s32[]{:S(2)}) async-start(), calls=%async_computation.20 | async-start | bytes 1769472 | tf_op jit(solution)/shard_map/all_gather | solution.py:26
  74.7 3.4 collective-permute-start
  99.2 68.8 %all-gather.21.cloned.1.call-start = ((), (), s32[]{:S(2)}) async-start(), calls=%async_computation.10 | async-start | bytes 1327104 | tf_op jit(solution)/shard_map/all_gather | solution.py:174
  100.0 141.1 %all-reduce.67.cloned.1.call-start = ((), (), s32[]{:S(2)}) async-start(), calls=%async_computation.11 | async-start | bytes 3145728 | tf_op jit(solution)/shard_map/psum | solution.py:276
  174.5 91.5 %all-gather.23.cloned.1.call-start = ((), (), s32[]{:S(2)}) async-start(), calls=%async_computation.12 | async-start | bytes 1327104 | tf_op jit(solution)/shard_map/all_gather | solution.py:170
  175.1 117.3 %all-gather.25.cloned.1.call-start = ((), (), s32[]{:S(2)}) async-start(), calls=%async_computation.13 | async-start | bytes 1327104 | tf_op jit(solution)/shard_map/all_gather | solution.py:171
  175.8 183.8 %all-gather.31.cloned.1.call-start = ((), (), s32[]{:S(2)}) async-start(), calls=%async_computation.21 | async-start | bytes 1769472 | tf_op jit(solution)/shard_map/all_gather | solution.py:26
  303.1 3.5 collective-permute-start.1
  328.4 64.1 %all-gather.27.cloned.1.call-start = ((), (), s32[]{:S(2)}) async-start(), calls=%async_computation.14 | async-start | bytes 1327104 | tf_op jit(solution)/shard_map/all_gather | solution.py:174
  329.2 137.1 %all-gather.33.cloned.1.call-start = ((), (), s32[]{:S(2)}) async-start(), calls=%async_computation.22 | async-start | bytes 1769472 | tf_op jit(solution)/shard_map/all_gather | solution.py:26
  439.9 72.3 %reduce-scatter.17.cloned.1.call-start = ((), (), s32[]{:S(2)}) async-start(), calls=%async_computation.15 | async-start | bytes 655360 | tf_op jit(solution)/shard_map/reduce_scatter | solution.py:302
  491.6 111.4 %all-reduce.69.cloned.1.call-start = ((), (), s32[]{:S(2)}) async-start(), calls=%async_computation.16 | async-start | bytes 3145728 | tf_op jit(solution)/shard_map/psum | solution.py:310
  533.2 123.0 %all-gather.35.cloned.1.call-start = ((), (), s32[]{:S(2)}) async-start(), calls=%async_computation.23 | async-start | bytes 1769472 | tf_op jit(solution)/shard_map/all_gather | solution.py:26
  632.3 135.6 %reduce-scatter.19.cloned.1.call-start = ((), (), s32[]{:S(2)}) async-start(), calls=%async_computation.17 | async-start | bytes 655360 | tf_op jit(solution)/shard_map/reduce_scatter | solution.py:302
  681.1 131.4 %reduce-scatter.31.cloned.1.call-start = ((), (), s32[]{:S(2)}) async-start(), calls=%async_computation.27 | async-start | bytes 442368
  690.4 122.9 %reduce-scatter.27.cloned.1.call-start = ((), (), s32[]{:S(2)}) async-start(), calls=%async_computation.25 | async-start | bytes 442368
  694.0 138.0 %reduce-scatter.23.cloned.1.call-start = ((), (), s32[]{:S(2)}) async-start(), calls=%async_computation.19 | async-start | bytes 1327104 | tf_op jit(solution)/shard_map/reduce_scatter | solution.py:184
  699.6 155.1 %reduce-scatter.21.cloned.1.call-start = ((), (), s32[]{:S(2)}) async-start(), calls=%async_computation.18 | async-start | bytes 1327104 | tf_op jit(solution)/shard_map/reduce_scatter | solution.py:184
  750.5 141.2 %reduce-scatter.29.cloned.1.call-start = ((), (), s32[]{:S(2)}) async-start(), calls=%async_computation.26 | async-start | bytes 442368
  784.4 144.1 %reduce-scatter.25.cloned.1.call-start = ((), (), s32[]{:S(2)}) async-start(), calls=%async_computation.24 | async-start | bytes 442368
  786.4 232.3 %all-reduce.71.cloned.1.call-start = ((), (), s32[]{:S(2)}) async-start(), calls=%async_computation.28 | async-start | bytes 9437184
  799.1 343.8 %all-reduce.73.cloned.1.call-start = ((), (), s32[]{:S(2)}) async-start(), calls=%async_computation.29 | async-start | bytes 6291456 | tf_op jit(solution)/shard_map/psum | solution.py:276
  (266 other events, 3104.2 us)
Sparse Core Ops, SparseCore 0:
  10.5 27.6 all-gather.16
  40.7 23.9 all-gather.18
  99.3 29.2 all-gather.28
  131.0 23.9 all-gather.20
  174.6 66.4 all-reduce.66
  242.9 23.0 all-gather.22
  268.5 23.9 all-gather.24
  328.5 29.1 all-gather.30
  359.6 23.8 all-gather.26
  440.1 24.2 all-gather.32
  491.7 20.4 reduce-scatter.16
  533.3 69.6 all-reduce.68
  632.4 23.7 all-gather.34
  681.2 21.8 reduce-scatter.18
  706.0 32.2 reduce-scatter.30
  741.2 33.8 reduce-scatter.26
  778.1 36.7 reduce-scatter.22
  818.0 36.6 reduce-scatter.20
  857.7 33.9 reduce-scatter.28
  894.6 33.8 reduce-scatter.24
  932.0 86.6 all-reduce.70
  1021.7 121.1 all-reduce.72
where the time goes:
time: 1170 us; the launch traced here: 1150 us
  waiting for transfers between devices  468 us (40%)
  other arithmetic  187 us (16%)
  blocking collectives  180 us (15%)
  matrix products  174 us (15%)
  local copies, waits for them, and re-layouts  115 us (10%)
  between operations  20.8 us (2%)
    psum x2, waiting for transfers between devices, body(): hidden = hidden + lax.psum(partial_rows, 'head')  162 us
    unnamed x27, waiting for transfers between devices  126 us
    dot_general x30, matrix products, matmul_high(): jnp.dot(left, right, precision=lax.Precision.HIGHEST, preferred_element_t...  80.2 us
    psum x1, waiting for transfers between devices, body(): grad_branch, grad_ngain = lax.psum((grad_h_part, grad_ngain), 'head')  68.7 us
    another operation x29, other arithmetic  58.6 us
    all_gather x2, waiting for transfers between devices, fetch_weights(): lax.all_gather(parts[1], 'seq', axis=1, tiled=True)  47.4 us
    select_n x28, other arithmetic, hop(): jnp.where(position < mine, new, old)  45.6 us
    dot_general x12, matrix products, block_step(): jnp.einsum('hts,shp->thp', scores, per_head, precision=lax.Precision.HIGH...  35.9 us
  transfers between devices with their start and end apart: 26, of which 14 were waited for; matrix products, arithmetic and copies ran while one was open for 26% of the time, Pallas kernels for 0%

commit v1 on v0

v1 whole, which is shorter than its diff:
```python
from functools import partial

import jax
import jax.numpy as jnp
from jax import lax
from jax.sharding import PartitionSpec as P

STATE = 128
KERNEL = 4
BLOCK = 256


EPS = 1e-05
NEG_FILL = -1e30
EXACT = lax.Precision.HIGHEST
FAST = lax.Precision.HIGH


def passed_along(array, axis, by):
    count = lax.axis_size(axis)
    pairs = [(i, i + by) for i in range(count) if 0 <= i + by < count]
    return lax.ppermute(array, axis, pairs)


def product(spec, left, right, precision=FAST):
    return jnp.einsum(spec, left, right, precision=precision, preferred_element_type=jnp.float32)


def swish_act(values):
    return values * jax.nn.sigmoid(values)


def rms_scale(values):
    return lax.rsqrt(jnp.mean(values * values, axis=-1, keepdims=True) + EPS)


def segment_ids(doc_lengths, positions):
    ends = jnp.cumsum(doc_lengths)
    starts = ends - doc_lengths
    return jnp.sum((positions[:, None] >= starts[None, :]).astype(jnp.int32), axis=1) - 1


def widened(per_head, width):
    heads = per_head.shape[1]
    owner = jnp.arange(width) // (width // heads)
    spread = (jnp.arange(heads)[:, None] == owner[None, :]).astype(jnp.float32)
    return product("th,hc->tc", per_head, spread, EXACT)


def scaled_heads(state, factors):
    heads = factors.shape[0]
    return (state.reshape(heads, -1, state.shape[-1]) * factors[:, None, None]).reshape(state.shape)


def entering(pieces, decays, backward):
    count, mine = (lax.axis_size("seq"), lax.axis_index("seq"))
    order = jnp.arange(count)
    first, middle = (order[:, None], order[None, :])
    if backward:
        between = (middle > mine) & (middle < first)
        outside = order > mine
    else:
        between = (middle > first) & (middle < mine)
        outside = order < mine
    weights = jnp.prod(jnp.where(between[..., None], decays[None], 1.0), axis=1)
    weights = jnp.where(outside[:, None], weights, 0.0)
    heads = decays.shape[1]
    split = pieces.reshape(count, heads, -1, pieces.shape[-1])
    return jnp.sum(split * weights[:, :, None, None], axis=0).reshape(pieces.shape[1:])


def with_rows(rows, extra):
    width = rows.shape[1]
    more = -(-extra.shape[0] // (8 * width)) * 8
    return jnp.concatenate(
        [rows, jnp.pad(extra, (0, more * width - extra.shape[0])).reshape(more, width)], axis=0
    )


def front_fn(hidden, gain, weight_zx, weight_bd, inner_loc):
    normed = hidden * rms_scale(hidden) * gain[None, :]
    main = product("td,dc->tc", normed, weight_zx)
    side = product("td,dc->tc", normed, weight_bd)
    raw = jnp.concatenate([main[:, inner_loc:], side[:, : 2 * STATE]], axis=1)
    return (main[:, :inner_loc], raw, side[:, 2 * STATE :])


def conv_local(raw, prev_tail, kernel, bias, keeps):
    extended = jnp.concatenate([prev_tail, raw], axis=0)
    count = raw.shape[0]
    total = jnp.zeros_like(raw) + bias[None, :]
    for offset in range(KERNEL):
        total = total + kernel[offset][None, :] * extended[offset : offset + count] * keeps[offset]
    return swish_act(total)


def local_fn(values, dt_raw, dt_bias, a_log, skip_gain, bc, seg_now, seg_prev):
    count, width = values.shape
    heads = dt_raw.shape[1]
    rows = min(BLOCK, count)
    blocks = count // rows
    step_size = jax.nn.softplus(dt_raw + dt_bias)
    log_decay = -step_size * jnp.exp(a_log)
    order = jnp.arange(rows)
    lower = order[:, None] >= order[None, :]
    cum = product(
        "ts,bsh->bth",
        lower.astype(jnp.float32),
        log_decay.reshape(blocks, rows, heads),
        EXACT,
    )
    cum_rows = cum.transpose(2, 0, 1)
    seg = seg_now.reshape(blocks, rows)
    before = jnp.concatenate([seg_prev[None], seg[:-1, -1]])
    allowed = lower[None] & (seg[:, :, None] == seg[:, None, :])
    spans = cum_rows[:, :, :, None] - cum_rows[:, :, None, :]
    decays = jnp.exp(jnp.where(allowed[None], spans, NEG_FILL))
    b_matrix = bc[:, :STATE].reshape(blocks, rows, STATE)
    c_matrix = bc[:, STATE:].reshape(blocks, rows, STATE)
    scores = decays * product("btn,bsn->bts", c_matrix, b_matrix)[None]
    stepped = values * widened(step_size, width)
    output = product(
        "hbts,bshp->bthp", scores, stepped.reshape(blocks, rows, heads, width // heads)
    ).reshape(count, width)
    output = output + jnp.repeat(skip_gain, width // heads)[None, :] * values
    last = cum[:, -1]
    enter = jnp.exp(cum) * (seg == before[:, None]).astype(jnp.float32)[..., None]
    keep_end = (seg == seg[:, -1:]).astype(jnp.float32)
    leave = jnp.exp(last[:, None] - cum) * keep_end[..., None]
    weighted = stepped * widened(leave.reshape(count, heads), width)
    states = product("bsc,bsn->bcn", weighted.reshape(blocks, rows, width), b_matrix)
    carries = jnp.exp(last) * (seg[:, -1] == before).astype(jnp.float32)[:, None]
    state, decay = (states[0], carries[0])
    for block in range(1, blocks):
        state = scaled_heads(state, carries[block]) + states[block]
        decay = decay * carries[block]
    return (output, enter.reshape(count, heads), states, carries, state, decay)


def mix_fn(output, enter, states, carries, state_in, bc):
    count, width = output.shape
    blocks = states.shape[0]
    entry = [state_in]
    for block in range(blocks - 1):
        entry.append(scaled_heads(entry[-1], carries[block]) + states[block])
    c_matrix = bc[:, STATE:].reshape(blocks, count // blocks, STATE)
    read = product("btn,bcn->btc", c_matrix, jnp.stack(entry)).reshape(count, width)
    return output + widened(enter, width) * read


def gate_fn(mixed, gate_in, gate_gain, proj_out_loc):
    gated = mixed * swish_act(gate_in)
    rows = product("tc,dc->td", gated * gate_gain[None, :], proj_out_loc)
    return (rows, jnp.sum(gated * gated, axis=1))


def body(
    hidden_in,
    grad_out,
    doc_lengths,
    norm_gain,
    proj_z,
    proj_x,
    proj_bc,
    proj_dt,
    conv_x_kernel,
    conv_x_bias,
    conv_bc_kernel,
    conv_bc_bias,
    dt_bias,
    a_log,
    skip_gain,
    gate_gain,
    proj_out,
):
    count, width = hidden_in.shape
    layers, rows_loc, inner_loc = proj_z.shape
    bc_loc = proj_bc.shape[2]
    heads = proj_dt.shape[2]
    inner = inner_loc * lax.axis_size("head")
    bc_all = 2 * STATE
    margin = KERNEL - 1
    positions = lax.axis_index("seq") * count + jnp.arange(-margin, count, dtype=jnp.int32)
    seg_ext = segment_ids(doc_lengths, positions)
    seg_now = seg_ext[margin:]
    seg_prev = seg_ext[margin - 1]
    keeps = [
        (seg_ext[offset : offset + count] == seg_now).astype(jnp.float32)[:, None]
        for offset in range(KERNEL)
    ]

    def over_seq(part):
        return lax.all_gather(part, "seq", axis=0, tiled=True)

    columns = lax.all_gather(
        jnp.concatenate([proj_bc, conv_bc_kernel, conv_bc_bias[:, None]], axis=1),
        "head",
        axis=2,
        tiled=True,
    )
    first = over_seq(
        jnp.concatenate(
            [proj_z[0], proj_x[0]]
            + [
                part
                for layer in range(layers)
                for part in (columns[layer, :rows_loc], proj_dt[layer])
            ],
            axis=1,
        )
    )
    rest = over_seq(
        jnp.concatenate(
            [proj_out[0]]
            + [
                part
                for layer in range(1, layers)
                for part in (proj_z[layer], proj_x[layer], proj_out[layer])
            ],
            axis=1,
        )
    )
    full_zx = [first[:, : 2 * inner_loc]]
    full_out = [rest[:, :inner_loc]]
    for layer in range(1, layers):
        at = (3 * layer - 2) * inner_loc
        full_zx.append(rest[:, at : at + 2 * inner_loc])
        full_out.append(rest[:, at + 2 * inner_loc : at + 3 * inner_loc])
    side = first[:, 2 * inner_loc :]
    side_width = bc_all + heads
    full_bd = [side[:, layer * side_width : (layer + 1) * side_width] for layer in range(layers)]

    hidden = hidden_in
    saved = []
    for layer in range(layers):
        front_out, pull_front = jax.vjp(
            partial(front_fn, inner_loc=inner_loc),
            hidden,
            norm_gain[layer],
            full_zx[layer],
            full_bd[layer],
        )
        gate_in, raw, dt_raw = front_out
        prev_tail = passed_along(raw[count - margin :], "seq", 1)
        kernel = jnp.concatenate(
            [conv_x_kernel[layer], columns[layer, rows_loc : rows_loc + KERNEL]], axis=1
        )
        bias = jnp.concatenate([conv_x_bias[layer], columns[layer, rows_loc + KERNEL]])
        conv_out, pull_conv = jax.vjp(
            partial(conv_local, keeps=keeps), raw, prev_tail, kernel, bias
        )
        values, bc = (conv_out[:, :inner_loc], conv_out[:, inner_loc:])
        local_out, pull_local = jax.vjp(
            partial(local_fn, seg_now=seg_now, seg_prev=seg_prev),
            values,
            dt_raw,
            dt_bias[layer],
            a_log[layer],
            skip_gain[layer],
            bc,
        )
        output, enter, states, carries, state_dev, decay_dev = local_out
        packed = jnp.concatenate(
            [state_dev, jnp.pad(decay_dev[None], ((0, 7), (0, STATE - heads)))], axis=0
        )
        pieces = lax.all_gather(packed, "seq")
        decays = pieces[:, inner_loc, :heads]
        state_in = entering(pieces[:, :inner_loc], decays, False)
        mixed, pull_mix = jax.vjp(mix_fn, output, enter, states, carries, state_in, bc)
        (rows, squares), pull_gate = jax.vjp(
            gate_fn, mixed, gate_in, gate_gain[layer], full_out[layer]
        )
        if layer < layers - 1:
            summed = lax.psum(with_rows(rows, squares), "head")
            total_sq = summed[count:].reshape(-1)[:count]
            scale = lax.rsqrt(total_sq / inner + EPS)
            sums = summed[:count]
            hidden = hidden + scale[:, None] * sums
            grad_scale = sums
        else:
            pair = lax.psum(
                jnp.stack([squares, jnp.sum(grad_out * rows, axis=1)]), "head"
            )
            total_sq, grad_scale = (pair[0], pair[1])
            scale = lax.rsqrt(total_sq / inner + EPS)
            last_rows = scale[:, None] * rows
        saved.append(
            (
                pull_front,
                pull_conv,
                pull_local,
                pull_mix,
                pull_gate,
                scale,
                grad_scale,
                decays,
                state_in,
            )
        )

    grad_hidden = grad_out
    big, small = ([None] * layers for _ in range(2))
    own_bc = []
    for layer in reversed(range(layers)):
        (
            pull_front,
            pull_conv,
            pull_local,
            pull_mix,
            pull_gate,
            scale,
            grad_scale,
            decays,
            state_in,
        ) = saved[layer]
        if layer < layers - 1:
            grad_scale = jnp.sum(grad_hidden * grad_scale, axis=1)
        grad_squares = grad_scale * (-0.5 / inner) * scale * scale * scale
        grad_mixed, grad_gate_in, grad_ggain, grad_full_out = pull_gate(
            (scale[:, None] * grad_hidden, grad_squares)
        )
        grad_output, grad_enter, grad_states, grad_carries, grad_state_in, mix_bc = pull_mix(
            grad_mixed
        )
        grad_pieces = lax.all_gather(grad_state_in, "seq")
        if layer == layers - 1:
            grad_pieces, last_rows = lax.optimization_barrier((grad_pieces, last_rows))
            hidden_out = hidden + lax.psum(last_rows, "head")
        grad_state_end = entering(grad_pieces, decays, True)
        grad_decay = jnp.sum((grad_state_end * state_in).reshape(heads, -1), axis=1)
        grad_values, grad_dt_raw, grad_dbias, grad_alog, grad_skip, local_bc = pull_local(
            (grad_output, grad_enter, grad_states, grad_carries, grad_state_end, grad_decay)
        )
        grad_raw, grad_prev, grad_kernel, grad_cbias = pull_conv(
            jnp.concatenate([grad_values, mix_bc + local_bc], axis=1)
        )
        from_right = passed_along(grad_prev, "seq", -1)
        grad_raw = grad_raw + jnp.pad(from_right, ((count - margin, 0), (0, 0)))
        grad_part, grad_ngain, grad_zx, grad_bd = pull_front((grad_gate_in, grad_raw, grad_dt_raw))
        shared = jnp.concatenate(
            [grad_ngain, grad_kernel[:, inner_loc:].reshape(-1), grad_cbias[inner_loc:]]
        )
        if layer == layers - 1:
            grad_part, hidden_out = lax.optimization_barrier((grad_part, hidden_out))
        summed = lax.psum(with_rows(grad_part, shared), "head")
        grad_hidden = grad_hidden + summed[:count]
        shared = summed[count:].reshape(-1)[: shared.shape[0]]
        big[layer] = lax.psum_scatter(
            jnp.concatenate([grad_full_out, grad_zx, grad_bd], axis=1),
            "seq",
            scatter_dimension=0,
            tiled=True,
        )
        own_bc.append(
            lax.psum_scatter(
                big[layer][:, 3 * inner_loc : 3 * inner_loc + bc_all],
                "head",
                scatter_dimension=1,
                tiled=True,
            )
        )
        small[layer] = (
            grad_kernel[:, :inner_loc].reshape(-1),
            grad_cbias[:inner_loc],
            grad_ggain,
            grad_dbias,
            grad_alog,
            grad_skip,
            shared[:width],
            shared[width : width + KERNEL * bc_all],
            shared[width + KERNEL * bc_all :],
        )

    def laid_out(parts):
        sizes = [part.shape[0] for part in parts[0]]
        stacked = jnp.stack([jnp.concatenate(layer_parts) for layer_parts in parts])
        return (stacked, sizes)

    def taken(stacked, sizes):
        starts = [sum(sizes[:place]) for place in range(len(sizes))]
        return [stacked[:, start : start + size] for start, size in zip(starts, sizes)]

    stacked, sizes = laid_out(small)
    cxk, cxb, ggain, dbias, alog, skip, ngain, cbk, cbb = taken(lax.psum(stacked, "seq"), sizes)
    offset = lax.axis_index("head") * bc_loc
    cbk = lax.dynamic_slice_in_dim(cbk.reshape(layers, KERNEL, bc_all), offset, bc_loc, axis=2)
    cbb = lax.dynamic_slice_in_dim(cbb, offset, bc_loc, axis=1)
    return (
        hidden_out,
        grad_hidden,
        ngain,
        jnp.stack([part[:, inner_loc : 2 * inner_loc] for part in big]),
        jnp.stack([part[:, 2 * inner_loc : 3 * inner_loc] for part in big]),
        jnp.stack(own_bc[::-1]),
        jnp.stack([part[:, 3 * inner_loc + bc_all :] for part in big]),
        cxk.reshape(layers, KERNEL, inner_loc),
        cxb,
        cbk,
        cbb,
        dbias,
        alog,
        skip,
        ggain,
        jnp.stack([part[:, :inner_loc] for part in big]),
    )


def solution(mesh):
    in_specs = (
        P("seq", None),
        P("seq", None),
        P(),
        P(),
        P(None, "seq", "head"),
        P(None, "seq", "head"),
        P(None, "seq", "head"),
        P(None, "seq", "head"),
        P(None, None, "head"),
        P(None, "head"),
        P(None, None, "head"),
        P(None, "head"),
        P(None, "head"),
        P(None, "head"),
        P(None, "head"),
        P(None, "head"),
        P(None, "seq", "head"),
    )
    out_specs = (
        P("seq", None),
        P("seq", None),
        P(),
        P(None, "seq", "head"),
        P(None, "seq", "head"),
        P(None, "seq", "head"),
        P(None, "seq", "head"),
        P(None, None, "head"),
        P(None, "head"),
        P(None, None, "head"),
        P(None, "head"),
        P(None, "head"),
        P(None, "head"),
        P(None, "head"),
        P(None, "head"),
        P(None, "seq", "head"),
    )
    return jax.shard_map(body, mesh=mesh, in_specs=in_specs, out_specs=out_specs, check_vma=False)
```

time: 1170 us -> 834 us (0.71)
  blocking collectives: 180 us -> 51.5 us
  other arithmetic: 187 us -> 94.6 us
  waiting for transfers between devices: 468 us -> 382 us
  matrix products: 174 us -> 136 us
  local copies, waits for them, and re-layouts: 115 us -> 131 us
    unnamed x27 -> x16, waiting for transfers between devices: 126 us -> 25.4 us
    all_gather x8 -> x1, blocking collectives: 105 us -> 15.7 us  [body(): lax.all_gather(jnp.concatenate([proj_bc, conv_bc_kernel, conv_bc_bias[:,...]
    another operation x40 -> x10, other arithmetic: 59.3 us -> 4.59 us  [the longest x2 2.26 us: mix_fn(): jnp.stack(entry)]
    select_n x28 -> x4, other arithmetic: 45.6 us -> 2.49 us  [the longest x3 2.48 us: entering(): weights = jnp.where(outside[:, None], weights, 0.0)]
    psum x6 -> x2, blocking collectives: 74.8 us -> 35.9 us  [the longest x1 23.5 us: body(): lax.psum(stacked, 'seq')]
    dot_general x60 -> x58, matrix products: 174 us -> 136 us  [product(): jnp.einsum(spec, left, right, precision=precision, preferred_element_type...]
    reshape x10 -> x42, local copies, waits for them, and re-layouts: 3.03 us -> 37.2 us  [the longest x4 9.23 us: mix_fn(): product('btn,bcn->btc', c_matrix, jnp.stack(entry)).reshape(count, width)]
    broadcast_in_dim x42 -> x7, local copies, waits for them, and re-layouts: 30.1 us -> 3.77 us  [the longest x2 1.44 us: entering(): weights = jnp.prod(jnp.where(between[..., None], decays[None], 1.0), axis=1)]
  transfers between devices with their start and end apart: 26 -> 18, of which waited for: 14 -> 11; matrix products, arithmetic and copies ran while one was open for 26% -> 25% of each run, Pallas kernels for 0% -> 0%
where the time goes in v1:
time: 834 us; the launch traced here: 822 us
  waiting for transfers between devices  382 us (46%)
  matrix products  136 us (16%)
  local copies, waits for them, and re-layouts  131 us (16%)
  other arithmetic  94.6 us (11%)
  blocking collectives  51.5 us (6%)
  between operations  17.4 us (2%)
  starting transfers between devices  9.89 us (1%)
    dot_general x58, matrix products, product(): jnp.einsum(spec, left, right, precision=precision, preferred_element_type...  136 us
    psum x2, waiting for transfers between devices, body(): summed = lax.psum(with_rows(grad_part, shared), 'head')  131 us
    psum x1, waiting for transfers between devices, body(): summed = lax.psum(with_rows(rows, squares), 'head')  67.9 us
    all_gather x2, waiting for transfers between devices, over_seq(): return lax.all_gather(part, 'seq', axis=0, tiled=True)  53.9 us
    unnamed x524, local copies, waits for them, and re-layouts  42.1 us
    psum x1, waiting for transfers between devices, body(): hidden_out = hidden + lax.psum(last_rows, 'head')  35.7 us
    reduce_scatter x2, waiting for transfers between devices, body(): lax.psum_scatter(big[layer][:, 3 * inner_loc:3 * inner_loc + bc_all], 'he...  34.1 us
    all_gather x2, waiting for transfers between devices, body(): pieces = lax.all_gather(packed, 'seq')  33.8 us
  transfers between devices with their start and end apart: 18, of which 11 were waited for; matrix products, arithmetic and copies ran while one was open for 25% of the time, Pallas kernels for 0%

profile of v1, /device:TPU:0, one launch (start us, length us, event | category | flops | bytes accessed | tf_op | source)
XLA Modules:
  0.0 822.2 jit_solution(18058968250045826087)
XLA Ops:
  10.9 15.7 %all_gather.29 = f32[2,101,256]{1,0,2:T(2,128)S(1)} all-gather(f32[2,101,64]{1,0,2:T(2,128)S(1)} %pad_maximum_fusion.19), channel_id=1, replica_groups=mesh['seq'=8,'head'=4] {'head'}, dimensions={2}, use_global_device_ids=true | all-gather | bytes 258560 | tf_op jit(solution)/shard_map/all_gather | solution.py:195
  34.5 4.4 slice_reduce_fusion.1
  42.0 25.6 %all-gather.9.cloned.1.call-done = f32[768,1292]{1,0:T(8,128)} async-done(((f32[96,1292]{1,0:T(8,128)}), f32[768,1292]{1,0:T(8,128)}) %all-gather.9.cloned.1.call-update) | async-done | bytes 3969040 | tf_op jit(solution)/shard_map/all_gather | solution.py:193
  107.2 17.9 %all-gather.17.cloned.1.call-done = f32[3136,128]{1,0:T(8,128)} async-done(((f32[392,128]{1,0:T(8,128)}), f32[3136,128]{1,0:T(8,128)}) %all-gather.17.cloned.1.call-update) | async-done | bytes 1605648 | tf_op jit(solution)/shard_map/all_gather | solution.py:266
  133.5 4.0 multiply_reduce_fusion.23
  137.5 28.3 %all-gather.11.cloned.1.call-done = f32[768,1536]{1,0:T(8,128)} async-done(((f32[96,1536]{1,0:T(8,128)}), f32[768,1536]{1,0:T(8,128)}) %all-gather.11.cloned.1.call-update) | async-done | bytes 4718608 | tf_op jit(solution)/shard_map/all_gather | solution.py:193
  173.0 67.9 %all-reduce.58.cloned.1.call-done = f32[520,768]{1,0:T(8,128)} async-done(((f32[520,768]{1,0:T(8,128)}), f32[520,768]{1,0:T(8,128)}) %all-reduce.58.cloned.1.call-update) | async-done | bytes 1597456 | tf_op jit(solution)/shard_map/psum | solution.py:274
  292.6 15.9 %all-gather.19.cloned.1.call-done = f32[3136,128]{1,0:T(8,128)} async-done(((f32[392,128]{1,0:T(8,128)}), f32[3136,128]{1,0:T(8,128)}) %all-gather.19.cloned.1.call-update) | async-done | bytes 1605648 | tf_op jit(solution)/shard_map/all_gather | solution.py:266
  328.6 4.9 multiply_reduce_fusion.7
  334.2 12.4 %psum.43 = f32[2,512]{1,0:T(2,128)} all-reduce(f32[2,512]{1,0:T(2,128)} %pad_maximum_fusion.25), channel_id=1, replica_groups=mesh['seq'=8,'head'=4] {'head'}, use_global_device_ids=true, to_apply=%region_12.14 | all-reduce | flops 1024 | bytes 8192 | tf_op jit(solution)/shard_map/psum | solution.py:281
  374.9 5.3 fusion.25
  420.7 4.9 fusion.89
  425.6 35.7 %all-reduce.60.cloned.1.call-done = f32[512,768]{1,0:T(8,128)} async-done(((f32[512,768]{1,0:T(8,128)}), f32[512,768]{1,0:T(8,128)}) %all-reduce.60.cloned.1.call-update) | async-done | bytes 1572880 | tf_op jit(solution)/shard_map/psum | solution.py:328
  461.3 8.4 %multiply_reduce_fusion.4 = (f32[768]{0:T(1024)S(1)}, f32[512]{0:T(512)S(1)}, f32[512,768]{1,0:T(8,128)}, f32[512,768]{1,0:T(8,128)S(1)}) fusion(f32[512,768]{1,0:T(8,128)S(1)} %get-tuple-element.205, f32[512]{0:T(512)S(1)} %fusion.283, f32[768]{0:T(1024)S(1)} %copy-done.112, f32[512,768]{1,0:T(8,128)} %all-reduce.60.cloned.1.call-done, ...), kind=kOutput, calls=%fused_computation.58 | convolution fusion | flops 1815476992 | bytes 11806720 | tf_op jit(solution)/shard_map/transpose(jvp(td,dc->tc))/dot_general | solution.py:26
  474.2 69.0 %all-reduce.62.cloned.1.call-done = f32[520,768]{1,0:T(8,128)} async-done(((f32[520,768]{1,0:T(8,128)}), f32[520,768]{1,0:T(8,128)}) %all-reduce.62.cloned.1.call-update) | async-done | bytes 1597456 | tf_op jit(solution)/shard_map/psum | solution.py:345
  569.6 5.9 copy.495
  581.0 5.3 fusion.27
  624.5 4.4 multiply_reduce_fusion.1
  640.6 6.0 copy.493
  654.0 62.4 %all-reduce.64.cloned.1.call-done = f32[520,768]{1,0:T(8,128)} async-done(((f32[520,768]{1,0:T(8,128)}), f32[520,768]{1,0:T(8,128)}) %all-reduce.64.cloned.1.call-update) | async-done | bytes 1597456 | tf_op jit(solution)/shard_map/psum | solution.py:345
  717.2 23.5 %psum.47 = f32[2,4370]{1,0:T(2,128)S(1)} all-reduce(f32[2,4370]{1,0:T(2,128)S(1)} %pad_maximum_fusion.21), channel_id=1, replica_groups=mesh['seq'=8,'head'=4] {'seq'}, use_global_device_ids=true, to_apply=%region_65.67 | all-reduce | flops 8740 | bytes 69920 | tf_op jit(solution)/shard_map/psum | solution.py:384
  747.5 25.1 %reduce-scatter.13.cloned.1.call-done = f32[96,1414]{1,0:T(8,128)} async-done(((f32[768,1414]{1,0:T(8,128)}), f32[96,1414]{1,0:T(8,128)}) %reduce-scatter.13.cloned.1.call-update) | async-done | bytes 542992
  780.0 14.4 %reduce-scatter.11.cloned.1.call-done = f32[96,64]{0,1:T(8,128)} async-done(((f32[96,256]{0,1:T(8,128)}), f32[96,64]{0,1:T(8,128)}) %reduce-scatter.11.cloned.1.call-update) | async-done | bytes 24592 | tf_op jit(solution)/shard_map/reduce_scatter | solution.py:355
  794.3 19.8 %reduce-scatter.9.cloned.1.call-done = f32[96,64]{0,1:T(8,128)} async-done(((f32[96,256]{0,1:T(8,128)}), f32[96,64]{0,1:T(8,128)}) %reduce-scatter.9.cloned.1.call-update) | async-done | bytes 24592 | tf_op jit(solution)/shard_map/reduce_scatter | solution.py:355
  (886 shorter events, 317.9 us)
Async XLA Ops:
  7.2 60.3 %all-gather.9.cloned.1.call-start = ((), (), s32[]{:S(2)}) async-start(), calls=%async_computation.4 | async-start | bytes 4866048 | tf_op jit(solution)/shard_map/all_gather | solution.py:193
  28.7 96.4 %all-gather.17.cloned.1.call-start = ((), (), s32[]{:S(2)}) async-start(), calls=%async_computation.14 | async-start | bytes 1806336 | tf_op jit(solution)/shard_map/all_gather | solution.py:266
  32.3 48.5 %copy-start.143 = (f32[640]{0:T(1024)}, f32[640]{0:T(1024)S(1)}, u32[]{:S(2)}) copy-start(f32[640]{0:T(1024)S(1)} %get-tuple-element.174) | copy-start | bytes 7684
  32.3 48.5 %copy-start.145 = (f32[640]{0:T(1024)}, f32[640]{0:T(1024)S(1)}, u32[]{:S(2)}) copy-start(f32[640]{0:T(1024)S(1)} %get-tuple-element.175) | copy-start | bytes 7684
  76.1 4.2 collective-permute-start
  94.1 71.7 %all-gather.11.cloned.1.call-start = ((), (), s32[]{:S(2)}) async-start(), calls=%async_computation.5 | async-start | bytes 5308416 | tf_op jit(solution)/shard_map/all_gather | solution.py:193
  97.2 143.7 %all-reduce.58.cloned.1.call-start = ((), (), s32[]{:S(2)}) async-start(), calls=%async_computation.6 | async-start | bytes 3194880 | tf_op jit(solution)/shard_map/psum | solution.py:274
  98.8 67.0 %copy-start.160 = (f32[384]{0:T(512)}, f32[384]{0:T(512)S(1)}, u32[]{:S(2)}) copy-start(f32[384]{0:T(512)S(1)} %get-tuple-element.185) | copy-start | bytes 4612
  99.6 283.5 %copy-start.113 = (pred[2,256,256]{2,1,0:T(8,128)(4,1)}, pred[2,256,256]{2,1,0:T(8,128)(4,1)S(1)}, u32[]{:S(2)}) copy-start(pred[2,256,256]{2,1,0:T(8,128)(4,1)S(1)} %compare_and_fusion) | copy-start | bytes 393220
  170.8 137.6 %all-gather.19.cloned.1.call-start = ((), (), s32[]{:S(2)}) async-start(), calls=%async_computation.15 | async-start | bytes 1806336 | tf_op jit(solution)/shard_map/all_gather | solution.py:266
  256.6 3.4 collective-permute-start.1
  278.2 111.5 %all-gather.13.cloned.1.call-start = ((), (), s32[]{:S(2)}) async-start(), calls=%async_computation.7 | async-start | bytes 1769472 | tf_op jit(solution)/shard_map/all_gather | solution.py:325
  362.5 98.8 %all-reduce.60.cloned.1.call-start = ((), (), s32[]{:S(2)}) async-start(), calls=%async_computation.8 | async-start | bytes 3145728 | tf_op jit(solution)/shard_map/psum | solution.py:328
  394.9 148.3 %all-reduce.62.cloned.1.call-start = ((), (), s32[]{:S(2)}) async-start(), calls=%async_computation.9 | async-start | bytes 3194880 | tf_op jit(solution)/shard_map/psum | solution.py:345
  413.5 5.6 collective-permute-start.2
  474.0 72.7 %copy-start.167 = (f32[512]{0:T(512)S(1)}, f32[512]{0:T(512)}, u32[]{:S(2)}) copy-start(f32[512]{0:T(512)} %copy-done.166) | copy-start | bytes 6148
  474.0 120.1 %all-gather.15.cloned.1.call-start = ((), (), s32[]{:S(2)}) async-start(), calls=%async_computation.10 | async-start | bytes 1769472 | tf_op jit(solution)/shard_map/all_gather | solution.py:325
  559.6 90.3 %reduce-scatter.15.cloned.1.call-start = ((), (), s32[]{:S(2)}) async-start(), calls=%async_computation.17 | async-start | bytes 5308416
  575.6 140.8 %all-reduce.64.cloned.1.call-start = ((), (), s32[]{:S(2)}) async-start(), calls=%async_computation.11 | async-start | bytes 3194880 | tf_op jit(solution)/shard_map/psum | solution.py:345
  616.9 4.6 collective-permute-start.3
  630.5 142.1 %reduce-scatter.13.cloned.1.call-start = ((), (), s32[]{:S(2)}) async-start(), calls=%async_computation.16 | async-start | bytes 5308416
  646.7 70.4 %copy-start.218 = (f32[384]{0:T(512)S(1)}, f32[384]{0:T(512)}, u32[]{:S(2)}) copy-start(f32[384]{0:T(512)} %get-tuple-element.215) | copy-start | bytes 4612
  646.7 147.6 %reduce-scatter.11.cloned.1.call-start = ((), (), s32[]{:S(2)}) async-start(), calls=%async_computation.13 | async-start | bytes 163840 | tf_op jit(solution)/shard_map/reduce_scatter | solution.py:355
  653.9 160.2 %reduce-scatter.9.cloned.1.call-start = ((), (), s32[]{:S(2)}) async-start(), calls=%async_computation.12 | async-start | bytes 163840 | tf_op jit(solution)/shard_map/reduce_scatter | solution.py:355
  (247 other events, 1378.1 us)
Sparse Core Ops, SparseCore 0:
  28.8 38.6 all-gather.8
  94.3 30.8 all-gather.16
  127.0 38.7 all-gather.10
  170.9 69.9 all-reduce.57
  278.4 30.0 all-gather.18
  362.6 22.7 all-gather.12
  395.1 66.2 all-reduce.59
  474.1 69.0 all-reduce.61
  559.7 24.6 all-gather.14
  587.7 56.1 reduce-scatter.14
  646.4 69.9 all-reduce.63
  719.6 52.8 reduce-scatter.12
  774.8 19.4 reduce-scatter.10
  796.4 17.6 reduce-scatter.8
